TPU v7x, 128 devices: a whole 4x4x4 slice. The times are simulated.
128 devices in a mesh: row: 8 (over y, core), col: 16 (over x, z).
Axes of the slice: x: 4, y: 4, z: 4, core: 2. Of those that a mesh axis runs over, the one named last changes fastest.
Arguments:
- points: bfloat16 [1048576, 768], P(('row', 'col')), may hold values from -6 to 6
- node_of_row: int32 [1048576], P(('row', 'col')), may hold values from 0 to 255, as said below
- init_axes: float32 [768, 8], replicated, may hold values from -0.21875 to 0.21875
Outputs:
- projected: float32 [8, 1048576], P(None, ('row', 'col'))
Inputs may be any that keep to these rules, and one draw needn't show every extreme that they name: `node_of_row`: never falls along the points; every one of the 256 nodes has at least 512 points; the points of one device belong to at most 8 nodes, and exactly 8 on some device; a node may cover many devices.
All inputs are finite; a program needn't handle non-finite values.
Results may differ from a plain program's by a relative error of at most 0.0035.
The roundings to bfloat16 on the way count: a program that leaves them out, or rounds other values in their place, can miss the bound.
Values sent between devices are 32-bit elements; how exact they have to be, the bound alone decides.
A program may use at most 128 MiB of HBM per device.

v0:
```python
import jax
import jax.numpy as jnp
from jax import lax
from jax.sharding import Mesh
from jax.sharding import PartitionSpec as P

AXES = 8
ITERS = 3
SPAN_MOST = 8
ROW_COL = ("row_0", "row_1", "col_0", "col_1")


def laid_out(blocks, dim):
    dims = list(blocks.shape[1:])
    dims[dim] *= blocks.shape[0]
    return jnp.moveaxis(blocks, 0, dim).reshape(dims)


def gather_in_order(value, axes, order):
    blocks = value[None]
    for k in order:
        blocks = lax.all_gather(blocks, axes[k], axis=0, tiled=True)
    block = [lax.axis_size(axes[k]) for k in reversed(order)]
    blocks = blocks.reshape(*block, *value.shape)
    turned = sorted(range(len(order)), key=lambda place: order[len(order) - 1 - place])
    return blocks.transpose(*turned, *range(len(order), blocks.ndim)).reshape(-1, *value.shape)


def whole_of(value, axes, order, dim):
    return laid_out(gather_in_order(value, axes, order), dim)


def orthonormal(moment):
    found = []
    for index in range(moment.shape[1]):
        vector = moment[:, index]
        for column in found:
            vector = vector - jnp.sum(column * vector) * column
        vector = vector / jnp.sqrt(jnp.sum(vector * vector))
        found.append(vector)
    return jnp.stack(found, 1)


def lifted_terms(block, frames, centre):
    offset = jnp.einsum("ld,ldk->lk", centre, frames, precision=lax.Precision.HIGHEST)
    flat_frames = frames.astype(jnp.bfloat16).transpose(1, 0, 2).reshape(frames.shape[1], -1)
    spread = jnp.dot(block, flat_frames, preferred_element_type=jnp.float32)
    return spread.reshape(block.shape[0], SPAN_MOST, AXES) - offset[None]


def local_moment(block, member, frames, centre):
    terms = lifted_terms(block, frames, centre)
    lifted = terms.astype(jnp.bfloat16) * member.astype(jnp.bfloat16)[:, :, None]
    moment = lax.dot_general(
        block,
        lifted.reshape(block.shape[0], -1),
        (((0,), (0,)), ((), ())),
        preferred_element_type=jnp.float32,
    )
    moment = moment.reshape(block.shape[1], SPAN_MOST, AXES).transpose(1, 0, 2)
    column_sums = jnp.sum(lifted.astype(jnp.float32), 0)
    return moment - centre[:, :, None] * column_sums[:, None, :]


def settle(pieces, first_node, last_node):
    span_count = last_node - first_node
    first_mark = first_node.astype(jnp.float32)
    last_mark = last_node.astype(jnp.float32)
    flat_parts = [piece.reshape(piece.shape[0], -1) for piece in pieces]
    head_rows = tuple((flat[0:1] for flat in flat_parts))
    tail_rows = tuple((lax.dynamic_slice_in_dim(flat, span_count, 1, 0) for flat in flat_parts))
    tail_only = tuple((jnp.where(span_count > 0, tail, 0.0) for tail in tail_rows))
    node_marks = jnp.stack([first_mark, last_mark]).reshape(1, 2)
    gathered = jax.tree.map(
        lambda part: whole_of(part, ROW_COL, (0, 2, 3, 1), 0), (node_marks,) + head_rows + tail_only
    )
    marks_all = gathered[0]
    count_parts = len(flat_parts)
    not_self = jnp.arange(marks_all.shape[0], dtype=jnp.int32) != lax.axis_index(ROW_COL)
    head_first = (not_self & (marks_all[:, 0] == first_mark))[:, None]
    tail_first = (not_self & (marks_all[:, 1] == first_mark))[:, None]
    head_last = (not_self & (marks_all[:, 0] == last_mark) & (last_node != first_node))[:, None]
    tail_last = (not_self & (marks_all[:, 1] == last_mark) & (last_node != first_node))[:, None]
    into_first = []
    into_last = []
    for index in range(count_parts):
        heads_all = gathered[1 + index]
        tails_all = gathered[1 + count_parts + index]
        into_first.append(
            jnp.sum(
                jnp.where(head_first, heads_all, 0.0) + jnp.where(tail_first, tails_all, 0.0),
                0,
                keepdims=True,
            )
        )
        into_last.append(
            jnp.sum(
                jnp.where(head_last, heads_all, 0.0) + jnp.where(tail_last, tails_all, 0.0),
                0,
                keepdims=True,
            )
        )
    slot_index = jnp.arange(SPAN_MOST, dtype=jnp.int32)[:, None]
    settled = []
    for piece, flat, add_first, add_last in zip(pieces, flat_parts, into_first, into_last):
        whole = (
            flat
            + jnp.where(slot_index == 0, add_first, 0.0)
            + jnp.where(slot_index == span_count, add_last, 0.0)
        )
        settled.append(whole.reshape(piece.shape))
    return settled


def shards(points, node_of_row, init_axes):
    row_count = points.shape[0]
    width = points.shape[1]
    first_node = node_of_row[0]
    last_node = node_of_row[-1]
    slot_index = jnp.arange(SPAN_MOST, dtype=jnp.int32)
    member = (node_of_row[:, None] - first_node == slot_index[None, :]).astype(jnp.float32)
    node_sums = lax.dot_general(
        member.astype(jnp.bfloat16),
        points,
        (((0,), (0,)), ((), ())),
        preferred_element_type=jnp.float32,
    )
    node_counts = jnp.sum(member, 0)
    node_sums, node_counts = settle([node_sums, node_counts], first_node, last_node)
    live_slot = slot_index <= last_node - first_node
    centre = node_sums / jnp.where(live_slot, node_counts, 1.0)[:, None]
    start_frames = jnp.broadcast_to(init_axes, (SPAN_MOST, width, AXES))
    frames = start_frames
    for repeat in range(ITERS):
        moment = local_moment(points, member, frames, centre)
        (moment,) = settle([moment], first_node, last_node)
        moment = jnp.where(live_slot[:, None, None], moment, start_frames)
        frames = jax.vmap(orthonormal)(moment)
    terms = lifted_terms(points, frames, centre)
    coords = jnp.sum(terms * member[:, :, None], 1)
    return coords.reshape(row_count, AXES).T


def solution(mesh):
    split = Mesh(mesh.devices.reshape(4, 2, 4, 4), ("row_0", "row_1", "col_0", "col_1"))
    return jax.shard_map(
        shards,
        mesh=split,
        in_specs=(P(ROW_COL, None), P(ROW_COL), P()),
        out_specs=P(None, ROW_COL),
        check_vma=False,
    )
```

profile of v0, /device:TPU:1, one launch (start us, length us, event | category | flops | bytes accessed | tf_op | source)
XLA Modules:
  0.0 663.5 jit_solution(4486327910379594088)
XLA Ops:
  18.7 9.5 %all-reduce.11 = (f32[8]{0:T(128)S(1)}, f32[4]{0:T(128)S(1)}, f32[4]{0:T(128)S(1)}) all-reduce(f32[8]{0:T(128)S(1)} %maximum_dynamic-update-slice_fusion, f32[4]{0:T(128)S(1)} %bitcast_dynamic-update-slice_fusion, f32[4]{0:T(128)S(1)} %get-tuple-element.206), channel_id=2, replica_groups=mesh['row_0'=4,'row_1'=2,'col_0'=4,'col_1'=4] {'row_0'}, use_global_device_ids=true, to_apply=%add | all-reduce | flops 16 | bytes 128
  36.8 10.2 %all_gather.146 = f32[64,1,2]{2,1,0:T(1,128)S(1)} all-gather(f32[16,1,2]{2,1,0:T(1,128)S(1)} %all_gather.145), channel_id=1, replica_groups=mesh['row_0'=4,'row_1'=2,'col_0'=4,'col_1'=4] {'col_1'}, dimensions={0}, use_global_device_ids=true | all-gather | bytes 640 | tf_op jit(solution)/shard_map/all_gather | solution.py:22
  47.0 9.7 %all_gather.147 = f32[128,1,2]{2,1,0:T(1,128)S(1)} all-gather(f32[64,1,2]{2,1,0:T(1,128)S(1)} %all_gather.146), channel_id=1, replica_groups=mesh['row_0'=4,'row_1'=2,'col_0'=4,'col_1'=4] {'row_1'}, dimensions={0}, use_global_device_ids=true | all-gather | bytes 1536 | tf_op jit(solution)/shard_map/all_gather | solution.py:22
  102.9 9.3 %all-gather.32 = f32[4,4,768]{2,1,0:T(4,128)S(1)} all-gather(f32[1,4,768]{2,1,0:T(4,128)S(1)} %copy.252), channel_id=8, replica_groups=mesh['row_0'=4,'row_1'=2,'col_0'=4,'col_1'=4] {'col_0'}, dimensions={0}, use_global_device_ids=true | all-gather | bytes 61440 | tf_op jit(solution)/shard_map/all_gather | solution.py:22
  112.2 9.2 %all-gather.7 = f32[64,768]{1,0:T(8,128)S(1)} all-gather(f32[16,768]{1,0:T(8,128)S(1)} %reshape.2644), channel_id=9, replica_groups=mesh['row_0'=4,'row_1'=2,'col_0'=4,'col_1'=4] {'col_1'}, dimensions={0}, use_global_device_ids=true | all-gather | bytes 245760 | tf_op jit(solution)/shard_map/all_gather | solution.py:22
  121.5 10.4 %all-gather.8 = f32[128,768]{1,0:T(8,128)S(1)} all-gather(f32[64,768]{1,0:T(8,128)S(1)} %all-gather.7), channel_id=10, replica_groups=mesh['row_0'=4,'row_1'=2,'col_0'=4,'col_1'=4] {'row_1'}, dimensions={0}, use_global_device_ids=true | all-gather | bytes 589824 | tf_op jit(solution)/shard_map/all_gather | solution.py:22
  141.1 9.3 %all-gather.30 = f32[4,4,768]{2,1,0:T(4,128)S(1)} all-gather(f32[1,4,768]{2,1,0:T(4,128)S(1)} %copy.250), channel_id=4, replica_groups=mesh['row_0'=4,'row_1'=2,'col_0'=4,'col_1'=4] {'col_0'}, dimensions={0}, use_global_device_ids=true | all-gather | bytes 61440 | tf_op jit(solution)/shard_map/all_gather | solution.py:22
  150.4 9.2 %all-gather.3 = f32[64,768]{1,0:T(8,128)S(1)} all-gather(f32[16,768]{1,0:T(8,128)S(1)} %reshape.2640), channel_id=5, replica_groups=mesh['row_0'=4,'row_1'=2,'col_0'=4,'col_1'=4] {'col_1'}, dimensions={0}, use_global_device_ids=true | all-gather | bytes 245760 | tf_op jit(solution)/shard_map/all_gather | solution.py:22
  159.6 10.9 %all-gather.4 = f32[128,768]{1,0:T(8,128)S(1)} all-gather(f32[64,768]{1,0:T(8,128)S(1)} %all-gather.3), channel_id=6, replica_groups=mesh['row_0'=4,'row_1'=2,'col_0'=4,'col_1'=4] {'row_1'}, dimensions={0}, use_global_device_ids=true | all-gather | bytes 589824 | tf_op jit(solution)/shard_map/all_gather | solution.py:22
  202.7 10.8 %all-gather.34 = f32[4,4,6144]{2,1,0:T(4,128)S(1)} all-gather(f32[1,4,6144]{2,1,0:T(4,128)S(1)} %copy.263), channel_id=20, replica_groups=mesh['row_0'=4,'row_1'=2,'col_0'=4,'col_1'=4] {'col_0'}, dimensions={0}, use_global_device_ids=true | all-gather | bytes 491520 | tf_op jit(solution)/shard_map/all_gather | solution.py:22
  223.9 10.9 %all_gather.165 = f32[16,1,6144]{2,1,0:T(1,128)} all-gather(f32[4,1,6144]{2,1,0:T(1,128)S(1)} %all_gather.164), channel_id=1, replica_groups=mesh['row_0'=4,'row_1'=2,'col_0'=4,'col_1'=4] {'col_0'}, dimensions={0}, use_global_device_ids=true | all-gather | bytes 491520 | tf_op jit(solution)/shard_map/all_gather | solution.py:22
  242.0 28.1 %all-gather.52.cloned.1.call-done = f32[64,1,6144]{2,1,0:T(1,128)} async-done(((f32[16,1,6144]{2,1,0:T(1,128)}), f32[64,1,6144]{2,1,0:T(1,128)}) %all-gather.52.cloned.1.call-update) | async-done | bytes 1572880 | tf_op jit(solution)/shard_map/all_gather | solution.py:22
  270.9 16.1 %all-gather.66.cloned.1.call-done = f32[128,6144]{1,0:T(8,128)} async-done(((f32[64,6144]{1,0:T(8,128)}), f32[128,6144]{1,0:T(8,128)}) %all-gather.66.cloned.1.call-update) | async-done | bytes 3145744 | tf_op jit(solution)/shard_map/all_gather | solution.py:22
  292.2 12.6 %all-gather.54.cloned.1.call-done = f32[128,1,6144]{2,1,0:T(1,128)} async-done(((f32[64,1,6144]{2,1,0:T(1,128)}), f32[128,1,6144]{2,1,0:T(1,128)}) %all-gather.54.cloned.1.call-update) | async-done | bytes 3145744 | tf_op jit(solution)/shard_map/all_gather | solution.py:22
  304.7 15.6 %fusion.30 = (f32[6144]{0:T(1024)}, f32[6144]{0:T(1024)}) fusion(f32[2,4,4,4,1,6144]{5,4,3,2,1,0:T(1,128)S(1)} %reshape.2690, pred[4,2,4,4]{0,2,3,1:T(4,128)(4,1)S(1)} %copy.251, f32[4,2,4,4,1,6144]{5,4,0,2,3,1:T(1,128)} %bitcast.468, pred[4,2,4,4]{0,2,3,1:T(4,128)(4,1)S(1)} %copy.249, pred[4,2,4,4]{0,2,3,1:T(4,128)(4,1)S(1)} %copy-done.6, ...), kind=kLoop, calls=%fused_computation.39 | loop fusion | flops 6279168 | bytes 6341120 | tf_op jit(solution)/shard_map/reduce_sum | solution.py:90
  350.5 9.9 %all-gather.35 = f32[4,1,6144]{2,1,0:T(1,128)S(1)} all-gather(f32[1,1,6144]{2,1,0:T(1,128)S(1)} %fusion.57), channel_id=23, replica_groups=mesh['row_0'=4,'row_1'=2,'col_0'=4,'col_1'=4] {'row_0'}, dimensions={0}, use_global_device_ids=true | all-gather | bytes 122880 | tf_op jit(solution)/shard_map/all_gather | solution.py:22
  360.5 9.9 %all-gather.36 = f32[4,4,6144]{2,1,0:T(4,128)S(1)} all-gather(f32[1,4,6144]{2,1,0:T(4,128)S(1)} %copy.274), channel_id=24, replica_groups=mesh['row_0'=4,'row_1'=2,'col_0'=4,'col_1'=4] {'col_0'}, dimensions={0}, use_global_device_ids=true | all-gather | bytes 491520 | tf_op jit(solution)/shard_map/all_gather | solution.py:22
  380.8 11.5 %all_gather.173 = f32[16,1,6144]{2,1,0:T(1,128)} all-gather(f32[4,1,6144]{2,1,0:T(1,128)S(1)} %all_gather.172), channel_id=1, replica_groups=mesh['row_0'=4,'row_1'=2,'col_0'=4,'col_1'=4] {'col_0'}, dimensions={0}, use_global_device_ids=true | all-gather | bytes 491520 | tf_op jit(solution)/shard_map/all_gather | solution.py:22
  392.4 10.7 %all-gather.68.cloned.1.call-done = f32[64,6144]{1,0:T(8,128)} async-done(((f32[16,6144]{1,0:T(8,128)}), f32[64,6144]{1,0:T(8,128)}) %all-gather.68.cloned.1.call-update) | async-done | bytes 1572880 | tf_op jit(solution)/shard_map/all_gather | solution.py:22
  403.1 28.0 %all-gather.56.cloned.1.call-done = f32[64,1,6144]{2,1,0:T(1,128)} async-done(((f32[16,1,6144]{2,1,0:T(1,128)}), f32[64,1,6144]{2,1,0:T(1,128)}) %all-gather.56.cloned.1.call-update) | async-done | bytes 1572880 | tf_op jit(solution)/shard_map/all_gather | solution.py:22
  431.2 16.8 %all-gather.70.cloned.1.call-done = f32[128,6144]{1,0:T(8,128)} async-done(((f32[64,6144]{1,0:T(8,128)}), f32[128,6144]{1,0:T(8,128)}) %all-gather.70.cloned.1.call-update) | async-done | bytes 3145744 | tf_op jit(solution)/shard_map/all_gather | solution.py:22
  453.2 12.7 %all-gather.58.cloned.1.call-done = f32[128,1,6144]{2,1,0:T(1,128)} async-done(((f32[64,1,6144]{2,1,0:T(1,128)}), f32[128,1,6144]{2,1,0:T(1,128)}) %all-gather.58.cloned.1.call-update) | async-done | bytes 3145744 | tf_op jit(solution)/shard_map/all_gather | solution.py:22
  465.9 15.6 %fusion.29 = (f32[6144]{0:T(1024)}, f32[6144]{0:T(1024)}) fusion(f32[2,4,4,4,1,6144]{5,4,3,2,1,0:T(1,128)S(1)} %reshape.2691, pred[4,2,4,4]{0,2,3,1:T(4,128)(4,1)S(1)} %copy.251, f32[4,2,4,4,1,6144]{5,4,0,2,3,1:T(1,128)} %bitcast.470, pred[4,2,4,4]{0,2,3,1:T(4,128)(4,1)S(1)} %copy.249, pred[4,2,4,4]{0,2,3,1:T(4,128)(4,1)S(1)} %copy-done.7, ...), kind=kLoop, calls=%fused_computation.38 | loop fusion | flops 6279168 | bytes 6341120 | tf_op jit(solution)/shard_map/reduce_sum | solution.py:90
  511.4 9.9 %all-gather.37 = f32[4,1,6144]{2,1,0:T(1,128)S(1)} all-gather(f32[1,1,6144]{2,1,0:T(1,128)S(1)} %fusion.58), channel_id=27, replica_groups=mesh['row_0'=4,'row_1'=2,'col_0'=4,'col_1'=4] {'row_0'}, dimensions={0}, use_global_device_ids=true | all-gather | bytes 122880 | tf_op jit(solution)/shard_map/all_gather | solution.py:22
  521.3 9.9 %all-gather.38 = f32[4,4,6144]{2,1,0:T(4,128)S(1)} all-gather(f32[1,4,6144]{2,1,0:T(4,128)S(1)} %copy.283), channel_id=28, replica_groups=mesh['row_0'=4,'row_1'=2,'col_0'=4,'col_1'=4] {'col_0'}, dimensions={0}, use_global_device_ids=true | all-gather | bytes 491520 | tf_op jit(solution)/shard_map/all_gather | solution.py:22
  541.7 11.5 %all_gather.181 = f32[16,1,6144]{2,1,0:T(1,128)} all-gather(f32[4,1,6144]{2,1,0:T(1,128)S(1)} %all_gather.180), channel_id=1, replica_groups=mesh['row_0'=4,'row_1'=2,'col_0'=4,'col_1'=4] {'col_0'}, dimensions={0}, use_global_device_ids=true | all-gather | bytes 491520 | tf_op jit(solution)/shard_map/all_gather | solution.py:22
  553.3 10.7 %all-gather.72.cloned.1.call-done = f32[64,6144]{1,0:T(8,128)} async-done(((f32[16,6144]{1,0:T(8,128)}), f32[64,6144]{1,0:T(8,128)}) %all-gather.72.cloned.1.call-update) | async-done | bytes 1572880 | tf_op jit(solution)/shard_map/all_gather | solution.py:22
  564.0 28.0 %all-gather.60.cloned.1.call-done = f32[64,1,6144]{2,1,0:T(1,128)} async-done(((f32[16,1,6144]{2,1,0:T(1,128)}), f32[64,1,6144]{2,1,0:T(1,128)}) %all-gather.60.cloned.1.call-update) | async-done | bytes 1572880 | tf_op jit(solution)/shard_map/all_gather | solution.py:22
  592.0 16.9 %all-gather.74.cloned.1.call-done = f32[128,6144]{1,0:T(8,128)} async-done(((f32[64,6144]{1,0:T(8,128)}), f32[128,6144]{1,0:T(8,128)}) %all-gather.74.cloned.1.call-update) | async-done | bytes 3145744 | tf_op jit(solution)/shard_map/all_gather | solution.py:22
  614.1 12.6 %all-gather.62.cloned.1.call-done = f32[128,1,6144]{2,1,0:T(1,128)} async-done(((f32[64,1,6144]{2,1,0:T(1,128)}), f32[128,1,6144]{2,1,0:T(1,128)}) %all-gather.62.cloned.1.call-update) | async-done | bytes 3145744 | tf_op jit(solution)/shard_map/all_gather | solution.py:22
  626.7 15.0 %fusion.28 = (f32[6144]{0:T(1024)S(1)}, f32[6144]{0:T(1024)S(1)}) fusion(f32[2,4,4,4,1,6144]{5,4,3,2,1,0:T(1,128)S(1)} %reshape.2692, pred[4,2,4,4]{0,2,3,1:T(4,128)(4,1)S(1)} %copy.251, f32[4,2,4,4,1,6144]{5,4,0,2,3,1:T(1,128)} %bitcast.469, pred[4,2,4,4]{0,2,3,1:T(4,128)(4,1)S(1)} %copy.249, pred[4,2,4,4]{0,2,3,1:T(4,128)(4,1)S(1)} %copy-done.8, ...), kind=kLoop, calls=%fused_computation.37 | loop fusion | flops 6279168 | bytes 6341120 | tf_op jit(solution)/shard_map/reduce_sum | solution.py:90
  647.3 9.2 %fusion.31 = f32[8192,8]{0,1:T(8,128)} fusion(bf16[8192,768]{1,0:T(8,128)(2,1)} %param.3, f32[8192,8]{0,1:T(8,128)S(1)} %copy-done, f32[8,8]{1,0:T(8,128)S(1)} %bitcast.480, bf16[768,8,8]{0,1,2:T(8,128)(2,1)S(1)} %convert_bitcast_fusion), kind=kOutput, calls=%fused_computation.43 | convolution fusion | flops 806813696 | bytes 13205760 | tf_op jit(solution)/shard_map/dot_general | solution.py:47
  (306 shorter events, 221.1 us)
Async XLA Ops:
  6.5 235.4 %all-gather.64.cloned.1.call-start = ((), (), s32[]{:S(2)}) async-start(), calls=%async_computation.6 | async-start | bytes 1966080 | tf_op jit(solution)/shard_map/all_gather | solution.py:22
  14.0 161.5 %copy-start.15 = (pred[8]{0:T(512)(128)(4,1)}, pred[8]{0:T(512)(128)(4,1)S(1)}, u32[]{:S(2)}) copy-start(pred[8]{0:T(512)(128)(4,1)S(1)} %iota_compare_fusion.1) | copy-start | bytes 28
  14.0 161.5 %copy-start.17 = (pred[8]{0:T(512)(128)(4,1)}, pred[8]{0:T(512)(128)(4,1)S(1)}, u32[]{:S(2)}) copy-start(pred[8]{0:T(512)(128)(4,1)S(1)} %iota_compare_fusion.3) | copy-start | bytes 28
  93.8 81.8 %copy-start.1 = (f32[768,8]{0,1:T(8,128)S(1)}, f32[768,8]{0,1:T(8,128)}, u32[]{:S(2)}) copy-start(f32[768,8]{0,1:T(8,128)} %param.5) | copy-start | bytes 73732
  172.7 12.1 %copy-start.5 = (pred[4,2,4,4]{0,2,3,1:T(4,128)(4,1)}, pred[4,2,4,4]{0,2,3,1:T(4,128)(4,1)S(1)}, u32[]{:S(2)}) copy-start(pred[4,2,4,4]{0,2,3,1:T(4,128)(4,1)S(1)} %copy.254) | copy-start | bytes 388
  173.0 11.8 %copy-start.9 = (pred[4,2,4,4]{0,2,3,1:T(4,128)(4,1)}, pred[4,2,4,4]{0,2,3,1:T(4,128)(4,1)S(1)}, u32[]{:S(2)}) copy-start(pred[4,2,4,4]{0,2,3,1:T(4,128)(4,1)S(1)} %copy.253) | copy-start | bytes 388
  175.0 9.8 %slice-start = ((s8[12582912]{0:T(1024)(128)(4,1)}), s8[4194304]{0:T(1024)(128)(4,1)S(1)}, s32[]{:S(2)}) async-start(s8[12582912]{0:T(1024)(128)(4,1)} %bitcast.466), calls=%async_computation.12 | async-start | bytes 8388608
  175.6 9.2 %copy-start.2 = (f32[8,768,1]{1,2,0:T(1,128)}, f32[8,768,1]{1,2,0:T(1,128)S(1)}, u32[]{:S(2)}) copy-start(f32[8,768,1]{1,2,0:T(1,128)S(1)} %copy.288) | copy-start | bytes 73732
  176.1 8.8 %slice-start.2 = ((s8[12582912]{0:T(1024)(128)(4,1)}), s8[4194304]{0:T(1024)(128)(4,1)S(1)}, s32[]{:S(2)}) async-start(s8[12582912]{0:T(1024)(128)(4,1)} %bitcast.466), calls=%async_computation.14 | async-start | bytes 8388608
  189.9 24.6 %slice-start.4 = ((f32[8,768,8]{1,0,2:T(8,128)}), f32[1,768,8]{1,0,2:T(1,128)S(1)}, s32[]{:S(2)}) async-start(f32[8,768,8]{1,0,2:T(8,128)} %bitcast_subtract_fusion.2), calls=%async_computation.16 | async-start | bytes 49152 | tf_op jit(solution)/shard_map/slice | solution.py:70
  214.4 55.7 %all-gather.52.cloned.1.call-start = ((), (), s32[]{:S(2)}) async-start(), calls=%async_computation | async-start | bytes 1966080 | tf_op jit(solution)/shard_map/all_gather | solution.py:22
  234.9 52.1 %all-gather.66.cloned.1.call-start = ((), (), s32[]{:S(2)}) async-start(), calls=%async_computation.7 | async-start | bytes 4718592 | tf_op jit(solution)/shard_map/all_gather | solution.py:22
  241.9 62.8 %all-gather.54.cloned.1.call-start = ((), (), s32[]{:S(2)}) async-start(), calls=%async_computation.1 | async-start | bytes 4718592 | tf_op jit(solution)/shard_map/all_gather | solution.py:22
  270.1 132.9 %all-gather.68.cloned.1.call-start = ((), (), s32[]{:S(2)}) async-start(), calls=%async_computation.8 | async-start | bytes 1966080 | tf_op jit(solution)/shard_map/all_gather | solution.py:22
  270.9 33.8 %copy-start.6 = (pred[4,2,4,4]{0,2,3,1:T(4,128)(4,1)S(1)}, pred[4,2,4,4]{0,2,3,1:T(4,128)(4,1)}, u32[]{:S(2)}) copy-start(pred[4,2,4,4]{0,2,3,1:T(4,128)(4,1)} %copy-done.5) | copy-start | bytes 388
  270.9 33.8 %copy-start.10 = (pred[4,2,4,4]{0,2,3,1:T(4,128)(4,1)S(1)}, pred[4,2,4,4]{0,2,3,1:T(4,128)(4,1)}, u32[]{:S(2)}) copy-start(pred[4,2,4,4]{0,2,3,1:T(4,128)(4,1)} %copy-done.9) | copy-start | bytes 388
  346.8 24.5 %slice-start.5 = ((f32[8,768,8]{1,0,2:T(8,128)}), f32[1,768,8]{1,0,2:T(1,128)S(1)}, s32[]{:S(2)}) async-start(f32[8,768,8]{1,0,2:T(8,128)} %bitcast_subtract_fusion.1), calls=%async_computation.17 | async-start | bytes 49152 | tf_op jit(solution)/shard_map/slice | solution.py:70
  371.3 59.8 %all-gather.56.cloned.1.call-start = ((), (), s32[]{:S(2)}) async-start(), calls=%async_computation.2 | async-start | bytes 1966080 | tf_op jit(solution)/shard_map/all_gather | solution.py:22
  392.3 55.7 %all-gather.70.cloned.1.call-start = ((), (), s32[]{:S(2)}) async-start(), calls=%async_computation.9 | async-start | bytes 4718592 | tf_op jit(solution)/shard_map/all_gather | solution.py:22
  403.1 62.8 %all-gather.58.cloned.1.call-start = ((), (), s32[]{:S(2)}) async-start(), calls=%async_computation.3 | async-start | bytes 4718592 | tf_op jit(solution)/shard_map/all_gather | solution.py:22
  431.1 34.8 %copy-start.7 = (pred[4,2,4,4]{0,2,3,1:T(4,128)(4,1)S(1)}, pred[4,2,4,4]{0,2,3,1:T(4,128)(4,1)}, u32[]{:S(2)}) copy-start(pred[4,2,4,4]{0,2,3,1:T(4,128)(4,1)} %copy-done.5) | copy-start | bytes 388
  431.1 34.7 %copy-start.11 = (pred[4,2,4,4]{0,2,3,1:T(4,128)(4,1)S(1)}, pred[4,2,4,4]{0,2,3,1:T(4,128)(4,1)}, u32[]{:S(2)}) copy-start(pred[4,2,4,4]{0,2,3,1:T(4,128)(4,1)} %copy-done.9) | copy-start | bytes 388
  431.1 132.8 %all-gather.72.cloned.1.call-start = ((), (), s32[]{:S(2)}) async-start(), calls=%async_computation.10 | async-start | bytes 1966080 | tf_op jit(solution)/shard_map/all_gather | solution.py:22
  507.7 24.5 %slice-start.3 = ((f32[8,768,8]{1,0,2:T(8,128)}), f32[1,768,8]{1,0,2:T(1,128)S(1)}, s32[]{:S(2)}) async-start(f32[8,768,8]{1,0,2:T(8,128)} %bitcast_subtract_fusion), calls=%async_computation.15 | async-start | bytes 49152 | tf_op jit(solution)/shard_map/slice | solution.py:70
  532.2 59.8 %all-gather.60.cloned.1.call-start = ((), (), s32[]{:S(2)}) async-start(), calls=%async_computation.4 | async-start | bytes 1966080 | tf_op jit(solution)/shard_map/all_gather | solution.py:22
  553.3 55.7 %all-gather.74.cloned.1.call-start = ((), (), s32[]{:S(2)}) async-start(), calls=%async_computation.11 | async-start | bytes 4718592 | tf_op jit(solution)/shard_map/all_gather | solution.py:22
  564.0 62.7 %all-gather.62.cloned.1.call-start = ((), (), s32[]{:S(2)}) async-start(), calls=%async_computation.5 | async-start | bytes 4718592 | tf_op jit(solution)/shard_map/all_gather | solution.py:22
  592.0 34.6 %copy-start.8 = (pred[4,2,4,4]{0,2,3,1:T(4,128)(4,1)S(1)}, pred[4,2,4,4]{0,2,3,1:T(4,128)(4,1)}, u32[]{:S(2)}) copy-start(pred[4,2,4,4]{0,2,3,1:T(4,128)(4,1)} %copy-done.5) | copy-start | bytes 388
  592.0 34.6 %copy-start.12 = (pred[4,2,4,4]{0,2,3,1:T(4,128)(4,1)S(1)}, pred[4,2,4,4]{0,2,3,1:T(4,128)(4,1)}, u32[]{:S(2)}) copy-start(pred[4,2,4,4]{0,2,3,1:T(4,128)(4,1)} %copy-done.9) | copy-start | bytes 388
  626.6 15.7 %copy-start.16 = (pred[8]{0:T(512)(128)(4,1)S(1)}, pred[8]{0:T(512)(128)(4,1)}, u32[]{:S(2)}) copy-start(pred[8]{0:T(512)(128)(4,1)} %copy-done.15) | copy-start | bytes 28
  626.6 15.7 %copy-start.18 = (pred[8]{0:T(512)(128)(4,1)S(1)}, pred[8]{0:T(512)(128)(4,1)}, u32[]{:S(2)}) copy-start(pred[8]{0:T(512)(128)(4,1)} %copy-done.17) | copy-start | bytes 28
  626.6 15.7 %copy-start.19 = (pred[8]{0:T(512)(128)(4,1)S(1)}, pred[8]{0:T(512)(128)(4,1)}, u32[]{:S(2)}) copy-start(pred[8]{0:T(512)(128)(4,1)} %iota_compare_fusion.4) | copy-start | bytes 28
  (6 other events, 30.5 us)
Sparse Core Ops, SparseCore 0:
  214.5 27.3 all-gather.63
  243.6 26.4 all-gather.51
  271.8 15.2 all-gather.65
  288.5 16.1 all-gather.53
  371.4 31.5 all-gather.67
  404.6 26.4 all-gather.55
  432.7 15.2 all-gather.69
  449.7 16.1 all-gather.57
  532.3 31.6 all-gather.71
  565.5 26.4 all-gather.59
  593.7 15.2 all-gather.73
  610.4 16.1 all-gather.61
where the time goes:
time: 669 us; the launch traced here: 663 us
  blocking collectives  258 us (39%)
  waiting for transfers between devices  200 us (30%)
  other arithmetic  71.5 us (11%)
  matrix products  59.3 us (9%)
  local copies, waits for them, and re-layouts  52.6 us (8%)
  between operations  21.7 us (3%)
    all_gather x23, blocking collectives, gather_in_order(): blocks = lax.all_gather(blocks, axes[k], axis=0, tiled=True)  226 us
    all_gather x12, waiting for transfers between devices, gather_in_order(): blocks = lax.all_gather(blocks, axes[k], axis=0, tiled=True)  200 us
    reduce_sum x5, other arithmetic, settle(): jnp.sum(jnp.where(head_first, heads_all, 0.0) + jnp.where(tail_first, tai...  47.1 us
    dot_general x4, matrix products, lifted_terms(): spread = jnp.dot(block, flat_frames, preferred_element_type=jnp.float32)  35.1 us
    unnamed x4, blocking collectives  32 us
    reshape x8, local copies, waits for them, and re-layouts, gather_in_order(): blocks = blocks.reshape(*block, *value.shape)  16.1 us
    dot_general x3, matrix products, local_moment(): lax.dot_general(block, lifted.reshape(block.shape[0], -1), (((0,), (0,)),...  16 us
  transfers between devices with their start and end apart: 12, of which 12 were waited for; matrix products, arithmetic and copies ran while one was open for 3% of the time, Pallas kernels for 0%

commit v1 on v0

v1 whole, which is shorter than its diff:
```python
import functools

import jax
import jax.numpy as jnp
from jax import lax
from jax.experimental import pallas as pl
from jax.experimental.pallas import tpu as pltpu
from jax.sharding import PartitionSpec as P

AXES = 8
SLOTS = 8
WIDTH = 768
ROWS = 8192
COLS_N = 16
ROWS_N = 8
LANES = 128
TILES = WIDTH // LANES
LOAD = 1024
CHUNK = 2048
EXCHANGES = 3
f32 = jnp.float32
bf16 = jnp.bfloat16
NT = (((1,), (1,)), ((), ()))
NN = (((1,), (0,)), ((), ()))
MESH = pl.DeviceIdType.MESH


def split3(value):
    high = value.astype(bf16)
    rest = value - high.astype(f32)
    mid = rest.astype(bf16)
    low = (rest - mid.astype(f32)).astype(bf16)
    return jnp.concatenate([high, mid, low], 1)


def select_sum(weights, value):
    parts = lax.dot_general(weights, split3(value), NN, preferred_element_type=f32)
    return parts[:, :LANES] + parts[:, LANES : 2 * LANES] + parts[:, 2 * LANES :]


def kernel(
    points_ref,
    node_ref,
    init_ref,
    out_ref,
    x_ref,
    acc_ref,
    whole_ref,
    frame_ref,
    offset_ref,
    centre_ref,
    colsum_ref,
    mark_a,
    mark_b,
    mark_b_send,
    w_group,
    w_block,
    send_a,
    recv_a,
    send_b,
    recv_b,
    send_c,
    recv_c,
    load_sem,
    mark_sem,
    sem_a,
    sem_b,
    sem_c,
):
    row = lax.axis_index("row")
    col = lax.axis_index("col")

    def load(c):
        piece = pl.ds(c * LOAD, LOAD)
        return pltpu.make_async_copy(points_ref.at[piece, :], x_ref.at[piece, :], load_sem.at[c])

    for c in range(ROWS // LOAD):
        load(c).start()

    barrier = pltpu.get_barrier_semaphore()

    @pl.loop(1, COLS_N)
    def _(o):
        pl.semaphore_signal(
            barrier, inc=1, device_id=(row, lax.rem(col + o, COLS_N)), device_id_type=MESH
        )

    @pl.loop(1, ROWS_N)
    def _(o):
        pl.semaphore_signal(
            barrier, inc=1, device_id=(lax.rem(row + o, ROWS_N), col), device_id_type=MESH
        )

    def to_cols(source, target, sems):
        @pl.loop(1, COLS_N)
        def _(o):
            pltpu.make_async_remote_copy(
                src_ref=source(o),
                dst_ref=target(o),
                send_sem=sems.at[0],
                recv_sem=sems.at[1],
                device_id=(row, lax.rem(col + o, COLS_N)),
                device_id_type=MESH,
            ).start()

    def to_rows(source, target, sems):
        @pl.loop(1, ROWS_N)
        def _(o):
            pltpu.make_async_remote_copy(
                src_ref=source,
                dst_ref=target(o),
                send_sem=sems.at[0],
                recv_sem=sems.at[1],
                device_id=(lax.rem(row + o, ROWS_N), col),
                device_id_type=MESH,
            ).start()

    def settle(buffer, count, sem):
        some = buffer.at[pl.ds(1, count)]
        pltpu.make_async_copy(some, some, sem).wait()

    sub = lax.broadcasted_iota(jnp.int32, (8, LANES), 0)
    head_half = sub < 4
    first = jnp.broadcast_to(node_ref[0:1, 0:1], (8, LANES))
    last = jnp.broadcast_to(node_ref[0:1, ROWS - 1 : ROWS], (8, LANES))
    span = last - first
    mark_a[0] = jnp.where(head_half, first, last).astype(f32)

    base = init_ref[...].T
    base_bf = base.astype(bf16)
    base_pad = jnp.concatenate([base_bf, jnp.zeros_like(base_bf)], 0)
    acc_ref[...] = jnp.zeros_like(acc_ref)
    colsum_ref[...] = jnp.zeros_like(colsum_ref)

    def rel_of(start, size):
        ids = node_ref[:, pl.ds(start, size)]
        return jnp.broadcast_to(ids, (8, size)) - jnp.broadcast_to(first[:, 0:1], (8, size))

    def lane_sum(value):
        total = value[:, :LANES]
        for t in range(1, value.shape[1] // LANES):
            total = total + value[:, t * LANES : (t + 1) * LANES]
        return total

    def first_pass(c):
        load(c).wait()
        start = pl.multiple_of(c * LOAD, LOAD)
        x = x_ref[pl.ds(start, LOAD), :]
        s = lax.dot_general(base_pad, x, NT, preferred_element_type=f32)[:8]
        high = s.astype(bf16).astype(f32)
        low = s - high
        rel = rel_of(start, LOAD)
        sub_wide = lax.broadcasted_iota(jnp.int32, (8, LOAD), 0)
        member = jnp.where(rel == sub_wide, 1.0, 0.0)
        pieces = [jnp.where(rel == k, high, 0.0) for k in range(SLOTS)]
        pieces += [jnp.where(rel == k, low, 0.0) for k in range(SLOTS)]
        pieces += [member, jnp.zeros_like(member)]
        lifted = jnp.concatenate(pieces, 0).astype(bf16)
        acc_ref[...] += lax.dot_general(lifted, x, NN, preferred_element_type=f32)
        colsum_ref[0:8, :] += lane_sum(member)

    def first_range(lower, upper):
        @pl.loop(lower, upper)
        def _(c):
            first_pass(c)

    first_range(0, 2)
    pl.semaphore_wait(barrier, COLS_N - 1 + ROWS_N - 1)
    to_cols(lambda o: mark_a.at[0], lambda o: mark_a.at[o], mark_sem.at[0])
    first_range(2, 5)

    settle(mark_a, COLS_N - 1, mark_sem.at[0, 1])

    def voided(marks, count):
        other = pltpu.roll(marks, 4, 1)
        subs = lax.broadcasted_iota(jnp.int32, (count, 8, LANES), 1)
        return jnp.where((subs >= 4) & (marks == other), -1.0, marks)

    marks = mark_a[...]
    target = marks.reshape(LANES, LANES)
    sources = voided(marks, COLS_N).reshape(LANES, LANES).T
    like = (
        lax.rem(lax.broadcasted_iota(jnp.int32, (LANES, LANES), 0), 4)
        == lax.rem(lax.broadcasted_iota(jnp.int32, (LANES, LANES), 1), 4)
    )
    w_group[0:LANES, :] = jnp.where(like & (target == sources), 1.0, 0.0).astype(bf16)
    block_first = jnp.min(jnp.min(marks, 0), 0, keepdims=True)
    block_last = jnp.max(jnp.max(marks, 0), 0, keepdims=True)
    block_mark = jnp.where(head_half, block_first, block_last)
    block_rows = jnp.where(like[:8] & (block_mark == sources[:8]), 1.0, 0.0)
    w_group[LANES:, :] = jnp.concatenate([block_rows, jnp.zeros_like(block_rows)], 0).astype(bf16)
    mark_b_send[...] = block_mark
    mark_b[0] = jnp.full((8, LANES), -1.0, f32)
    to_rows(mark_b_send, lambda o: mark_b.at[o], mark_sem.at[1])
    first_range(5, 8)
    settle(mark_b, ROWS_N - 1, mark_sem.at[1, 1])
    marks_b = voided(mark_b[...], ROWS_N).reshape(8 * ROWS_N, LANES)
    marks_b = jnp.concatenate([marks_b, jnp.full((LANES - 8 * ROWS_N, LANES), -1.0, f32)], 0)
    block_sources = marks_b.T
    w_block[...] = jnp.where(like & (mark_a[...].reshape(LANES, LANES) == block_sources), 1.0, 0.0).astype(bf16)
    for e in range(EXCHANGES):
        recv_b[e, 0] = jnp.zeros((8, LANES), f32)

    def tile(t):
        return slice(t * LANES, (t + 1) * LANES)

    def spread_out(e, extra):
        head = acc_ref[0:8, :]
        tail = jnp.zeros_like(head)
        wide_span = jnp.broadcast_to(span[:, 0:1], (8, WIDTH))
        for k in range(1, SLOTS):
            tail = tail + jnp.where(wide_span == k, acc_ref[8 * k : 8 * k + 8, :], 0.0)
        for t in range(TILES):
            h, l = head[:, tile(t)], tail[:, tile(t)]
            send_a[e, 2 * t] = jnp.where(head_half, h, pltpu.roll(l, 4, 0))
            send_a[e, 2 * t + 1] = jnp.where(head_half, pltpu.roll(h, 4, 0), l)
        zero = jnp.zeros((8, LANES), f32)
        for m in range(2 * TILES, COLS_N):
            send_a[e, m] = zero
        if extra is not None:
            sums, counts = extra
            sub_wide = lax.broadcasted_iota(jnp.int32, (8, WIDTH), 0)
            sum_head = sums[0:1, :]
            sum_tail = jnp.sum(
                jnp.where((sub_wide == wide_span) & (sub_wide > 0), sums, 0.0), 0, keepdims=True
            )
            for t in range(TILES):
                m, r = 2 * TILES + t // 4, t % 4
                send_a[e, m, r : r + 1, :] = sum_head[:, tile(t)]
                send_a[e, m, r + 4 : r + 5, :] = sum_tail[:, tile(t)]
            count_head = counts[0:1, :]
            count_tail = jnp.sum(jnp.where((sub == span) & (sub > 0), counts, 0.0), 0, keepdims=True)
            send_a[e, 2 * TILES + 2] = jnp.where(
                head_half,
                jnp.broadcast_to(count_head, (8, LANES)),
                jnp.broadcast_to(count_tail, (8, LANES)),
            )

    def exchange(e):
        recv_a[e, 0] = send_a[e, col]
        to_cols(
            lambda o: send_a.at[e, lax.rem(col + o, COLS_N)],
            lambda o: recv_a.at[e, o],
            sem_a.at[e],
        )
        settle(recv_a.at[e], COLS_N - 1, sem_a.at[e, 1])
        group = select_sum(w_group[...], recv_a[e].reshape(LANES, LANES))
        send_b[e] = group[LANES : LANES + 8]
        to_rows(send_b.at[e], lambda o: recv_b.at[e, o], sem_b.at[e])
        settle(recv_b.at[e], ROWS_N - 1, sem_b.at[e, 1])
        blocks = recv_b[e].reshape(8 * ROWS_N, LANES)
        blocks = jnp.concatenate([blocks, jnp.zeros((LANES - 8 * ROWS_N, LANES), f32)], 0)
        whole = group[:LANES] + select_sum(w_block[...], blocks)
        send_c[e] = whole.reshape(COLS_N, 8, LANES)
        recv_c[e, col] = send_c[e, 0]
        @pl.loop(1, COLS_N)
        def _(o):
            pltpu.make_async_remote_copy(
                src_ref=send_c.at[e, o],
                dst_ref=recv_c.at[e, col],
                send_sem=sem_c.at[e, 0],
                recv_sem=sem_c.at[e, 1],
                device_id=(row, lax.rem(col - o + COLS_N, COLS_N)),
                device_id_type=MESH,
            ).start()
        settle(recv_c.at[e], COLS_N - 1, sem_c.at[e, 1])

    def gather_in(e):
        heads, tails = [], []
        for t in range(TILES):
            a, b = recv_c[e, 2 * t], recv_c[e, 2 * t + 1]
            heads.append(jnp.where(head_half, a, pltpu.roll(b, 4, 0)))
            tails.append(jnp.where(head_half, pltpu.roll(a, 4, 0), b))
        for t in range(TILES):
            whole_ref[t, 0:8, :] = heads[t]
            for k in range(1, SLOTS):
                whole_ref[t, 8 * k : 8 * k + 8, :] = jnp.where(
                    span == k, tails[t], acc_ref[8 * k : 8 * k + 8, tile(t)]
                )

    def take(k):
        return jnp.concatenate(
            [whole_ref[t, pl.ds(k, SLOTS, stride=AXES), :] for t in range(TILES)], 1
        )

    live = sub <= span

    def orthonormal(vectors):
        centre = centre_ref[...]
        for k in range(AXES):
            vector = vectors[k]
            square = jnp.sum(vector * vector, 1, keepdims=True)
            square = jnp.where(live[:, 0:1], square, 1.0)
            inverse = 1.0 / square
            for j in range(k + 1, AXES):
                along = jnp.sum(vector * vectors[j], 1, keepdims=True) * inverse
                vectors[j] = vectors[j] - along * vector
            unit = vector * (1.0 / jnp.sqrt(square))
            for t in range(TILES):
                frame_ref[t, pl.ds(k, SLOTS, stride=AXES), :] = unit[:, tile(t)]
            offset = jnp.sum(unit * centre, 1, keepdims=True)
            offset_ref[pl.ds(k, SLOTS, stride=AXES), :] = jnp.broadcast_to(offset, (8, LANES))

    acc_ref[0:64, :] = acc_ref[0:64, :] + acc_ref[64:128, :]
    counts = jnp.broadcast_to(jnp.sum(colsum_ref[0:8, :], 1, keepdims=True), (8, LANES))
    sums = acc_ref[128:136, :]
    spread_out(0, (sums, counts))
    exchange(0)
    gather_in(0)
    heads = [recv_c[0, 2 * TILES + t // 4, t % 4 : t % 4 + 1, :] for t in range(TILES)]
    tails = [recv_c[0, 2 * TILES + t // 4, t % 4 + 4 : t % 4 + 5, :] for t in range(TILES)]
    sub_wide = lax.broadcasted_iota(jnp.int32, (8, WIDTH), 0)
    wide_span = jnp.broadcast_to(span[:, 0:1], (8, WIDTH))
    sums = jnp.where(sub_wide == wide_span, jnp.concatenate(tails, 1), sums)
    sums = jnp.where(sub_wide == 0, jnp.concatenate(heads, 1), sums)
    counts = jnp.where(sub == span, recv_c[0, 2 * TILES + 2, 4:5, :], counts)
    counts = jnp.where(sub == 0, recv_c[0, 2 * TILES + 2, 0:1, :], counts)
    counts = jnp.where(live, counts, 1.0)
    centre = sums / counts[:, 0:1]
    centre_ref[...] = centre
    base_used = base_bf.astype(f32)
    vectors = []
    for k in range(AXES):
        total = jnp.sum(sums * base_used[k : k + 1, :], 1, keepdims=True)
        vectors.append(take(k) - total * centre)
    orthonormal(vectors)

    def frame_used():
        return jnp.concatenate([frame_ref[t] for t in range(TILES)], 1).astype(bf16)

    for e in range(1, EXCHANGES):
        frame = frame_used()
        acc_ref[0:64, :] = jnp.zeros((64, WIDTH), f32)
        colsum_ref[...] = jnp.zeros_like(colsum_ref)

        @pl.loop(0, ROWS // CHUNK)
        def _(c):
            start = pl.multiple_of(c * CHUNK, CHUNK)
            x = x_ref[pl.ds(start, CHUNK), :]
            s = lax.dot_general(frame, x, NT, preferred_element_type=f32)
            rel = rel_of(start, CHUNK)
            pieces = [
                jnp.where(
                    rel == k,
                    s[8 * k : 8 * k + 8]
                    - jnp.broadcast_to(offset_ref[8 * k : 8 * k + 8, 0:1], (8, CHUNK)),
                    0.0,
                )
                for k in range(SLOTS)
            ]
            lifted = jnp.concatenate(pieces, 0).astype(bf16)
            acc_ref[0:64, :] += lax.dot_general(lifted, x, NN, preferred_element_type=f32)
            colsum_ref[...] += lane_sum(lifted.astype(f32))

        column_sums = jnp.sum(colsum_ref[...], 1, keepdims=True)
        for k in range(SLOTS):
            acc_ref[8 * k : 8 * k + 8, :] -= column_sums[8 * k : 8 * k + 8] * centre_ref[k : k + 1, :]
        spread_out(e, None)
        exchange(e)
        gather_in(e)
        orthonormal([take(k) for k in range(AXES)])

    frame = frame_used()

    @pl.loop(0, ROWS // CHUNK)
    def _(c):
        start = pl.multiple_of(c * CHUNK, CHUNK)
        x = x_ref[pl.ds(start, CHUNK), :]
        s = lax.dot_general(frame, x, NT, preferred_element_type=f32)
        rel = rel_of(start, CHUNK)
        found = jnp.zeros((8, CHUNK), f32)
        for k in range(SLOTS):
            centred = s[8 * k : 8 * k + 8] - jnp.broadcast_to(
                offset_ref[8 * k : 8 * k + 8, 0:1], (8, CHUNK)
            )
            found = jnp.where(rel == k, centred, found)
        out_ref[:, pl.ds(start, CHUNK)] = found

    settle(mark_a, COLS_N - 1, mark_sem.at[0, 0])
    settle(mark_b, ROWS_N - 1, mark_sem.at[1, 0])
    for e in range(EXCHANGES):
        settle(recv_a.at[e], COLS_N - 1, sem_a.at[e, 0])
        settle(recv_b.at[e], ROWS_N - 1, sem_b.at[e, 0])
        settle(recv_c.at[e], COLS_N - 1, sem_c.at[e, 0])


def shards(points, node_of_row, init_axes):
    vmem = pl.BlockSpec(memory_space=pltpu.VMEM)
    DMA = pltpu.SemaphoreType.DMA
    return pl.pallas_call(
        kernel,
        out_shape=jax.ShapeDtypeStruct((AXES, ROWS), f32),
        in_specs=[pl.BlockSpec(memory_space=pl.ANY), vmem, vmem],
        out_specs=vmem,
        scratch_shapes=[
            pltpu.VMEM((ROWS, WIDTH), bf16),
            pltpu.VMEM((144, WIDTH), f32),
            pltpu.VMEM((TILES, 64, LANES), f32),
            pltpu.VMEM((TILES, 64, LANES), f32),
            pltpu.VMEM((64, LANES), f32),
            pltpu.VMEM((SLOTS, WIDTH), f32),
            pltpu.VMEM((64, LANES), f32),
            pltpu.VMEM((COLS_N, 8, LANES), f32),
            pltpu.VMEM((ROWS_N, 8, LANES), f32),
            pltpu.VMEM((8, LANES), f32),
            pltpu.VMEM((144, LANES), bf16),
            pltpu.VMEM((LANES, LANES), bf16),
            pltpu.VMEM((EXCHANGES, COLS_N, 8, LANES), f32),
            pltpu.VMEM((EXCHANGES, COLS_N, 8, LANES), f32),
            pltpu.VMEM((EXCHANGES, 8, LANES), f32),
            pltpu.VMEM((EXCHANGES, ROWS_N, 8, LANES), f32),
            pltpu.VMEM((EXCHANGES, COLS_N, 8, LANES), f32),
            pltpu.VMEM((EXCHANGES, COLS_N, 8, LANES), f32),
            DMA((ROWS // LOAD,)),
            DMA((2, 2)),
            DMA((EXCHANGES, 2)),
            DMA((EXCHANGES, 2)),
            DMA((EXCHANGES, 2)),
        ],
        compiler_params=pltpu.CompilerParams(
            collective_id=0, has_side_effects=True, vmem_limit_bytes=56 * 2**20
        ),
        name="principal_axes",
    )(points, node_of_row.reshape(1, ROWS), init_axes)


def solution(mesh):
    return jax.shard_map(
        shards,
        mesh=mesh,
        in_specs=(P(("row", "col"), None), P(("row", "col")), P()),
        out_specs=P(None, ("row", "col")),
        check_vma=False,
    )
```

time: 669 us -> 82.6 us (0.12)
  blocking collectives: 258 us -> 0 us
  waiting for transfers between devices: 200 us -> 0 us
  Pallas kernels: 0 us -> 79.1 us
  other arithmetic: 71.5 us -> 0 us
  matrix products: 59.3 us -> 0 us
  local copies, waits for them, and re-layouts: 52.6 us -> 3.31 us
  between operations: 21.7 us -> 0.01 us
    all_gather x23 -> x0, blocking collectives: 226 us -> none  [gather_in_order(): blocks = lax.all_gather(blocks, axes[k], axis=0, tiled=True)]
    all_gather x12 -> x0, waiting for transfers between devices: 200 us -> none  [gather_in_order(): blocks = lax.all_gather(blocks, axes[k], axis=0, tiled=True)]
    pallas_call x0 -> x1, Pallas kernels: none -> 79.1 us  [shards(): pl.pallas_call(kernel, out_shape=jax.ShapeDtypeStruct((AXES, ROWS), f32),...]
    dot_general x12 -> x0, matrix products: 59.3 us -> none  [the longest x4 35.1 us: lifted_terms(): spread = jnp.dot(block, flat_frames, preferred_element_type=jnp.float32)]
    reduce_sum x51 -> x0, other arithmetic: 57 us -> none  [the longest x5 47.1 us: settle(): jnp.sum(jnp.where(head_first, heads_all, 0.0) + jnp.where(tail_first, tai...]
    unnamed x4 -> x0, blocking collectives: 32 us -> none
    reshape x11 -> x0, local copies, waits for them, and re-layouts: 24.4 us -> none  [the longest x8 16.1 us: gather_in_order(): blocks = blocks.reshape(*block, *value.shape)]
    unnamed x77 -> x2, local copies, waits for them, and re-layouts: 11.3 us -> 3.31 us
  transfers between devices with their start and end apart: 12 -> 0, of which waited for: 12 -> 0; matrix products, arithmetic and copies ran while one was open for 3% -> 0% of each run, Pallas kernels for 0% -> 0%
where the time goes in v1:
time: 82.6 us; the launch traced here: 82.4 us
  Pallas kernels  79.1 us (96%)
  local copies, waits for them, and re-layouts  3.31 us (4%)
    pallas_call x1, Pallas kernels, shards(): pl.pallas_call(kernel, out_shape=jax.ShapeDtypeStruct((AXES, ROWS), f32),...  79.1 us
    unnamed x2, local copies, waits for them, and re-layouts  3.31 us

profile of v1, /device:TPU:1, one launch (start us, length us, event | category | flops | bytes accessed | tf_op | source)
XLA Modules:
  0.0 82.4 jit_solution(7657647733165404079)
XLA Ops:
  0.0 1.6 %copy.4.init_ref = f32[768,8]{1,0:T(8,128)} copy(f32[768,8]{0,1:T(8,128)} %param.5) | data formatting | bytes 49152 | tf_op args[2]
  1.6 79.1 %principal_axes.1 = f32[8,8192]{1,0:T(8,128)} custom-call(bf16[8192,768]{1,0:T(8,128)(2,1)} %points_ref.1, s32[1,8192]{1,0:T(1,128)} %bitcast.1, f32[768,8]{1,0:T(8,128)} %copy.4.init_ref), custom_call_target="tpu_custom_call" | custom-call | tf_op jit(solution)/shard_map/principal_axes/pallas_call | solution.py:390
  80.7 1.7 %copy.6 = f32[8,8192]{1,0:T(8,128)} copy(f32[8,8192]{1,0:T(8,128)} %principal_axes.1) | data formatting | bytes 524288

commit v2 on v1

--- a/solution.py
+++ b/solution.py
@@ -16,7 +16,7 @@
 LANES = 128
 TILES = WIDTH // LANES
 LOAD = 1024
-CHUNK = 2048
+CHUNK = 4096
 EXCHANGES = 3
 f32 = jnp.float32
 bf16 = jnp.bfloat16
@@ -33,8 +33,8 @@
     return jnp.concatenate([high, mid, low], 1)
 
 
-def select_sum(weights, value):
-    parts = lax.dot_general(weights, split3(value), NN, preferred_element_type=f32)
+def select_sum(weights, parts):
+    parts = lax.dot_general(weights, parts, NN, preferred_element_type=f32)
     return parts[:, :LANES] + parts[:, LANES : 2 * LANES] + parts[:, 2 * LANES :]
 
 
@@ -44,6 +44,7 @@
     init_ref,
     out_ref,
     x_ref,
+    xt_ref,
     acc_ref,
     whole_ref,
     frame_ref,
@@ -126,7 +127,7 @@
     span = last - first
     mark_a[0] = jnp.where(head_half, first, last).astype(f32)
 
-    base = init_ref[...].T
+    base = init_ref[...]
     base_bf = base.astype(bf16)
     base_pad = jnp.concatenate([base_bf, jnp.zeros_like(base_bf)], 0)
     acc_ref[...] = jnp.zeros_like(acc_ref)
@@ -146,7 +147,9 @@
         load(c).wait()
         start = pl.multiple_of(c * LOAD, LOAD)
         x = x_ref[pl.ds(start, LOAD), :]
-        s = lax.dot_general(base_pad, x, NT, preferred_element_type=f32)[:8]
+        xt = x.T
+        xt_ref[:, pl.ds(start, LOAD)] = xt
+        s = lax.dot_general(base_pad, xt, NN, preferred_element_type=f32)[:8]
         high = s.astype(bf16).astype(f32)
         low = s - high
         rel = rel_of(start, LOAD)
@@ -167,37 +170,40 @@
     first_range(0, 2)
     pl.semaphore_wait(barrier, COLS_N - 1 + ROWS_N - 1)
     to_cols(lambda o: mark_a.at[0], lambda o: mark_a.at[o], mark_sem.at[0])
-    first_range(2, 5)
-
-    settle(mark_a, COLS_N - 1, mark_sem.at[0, 1])
+    first_range(2, ROWS // LOAD)
+    like = (
+        lax.rem(lax.broadcasted_iota(jnp.int32, (LANES, LANES), 0), 4)
+        == lax.rem(lax.broadcasted_iota(jnp.int32, (LANES, LANES), 1), 4)
+    )
 
     def voided(marks, count):
         other = pltpu.roll(marks, 4, 1)
         subs = lax.broadcasted_iota(jnp.int32, (count, 8, LANES), 1)
         return jnp.where((subs >= 4) & (marks == other), -1.0, marks)
 
-    marks = mark_a[...]
-    target = marks.reshape(LANES, LANES)
-    sources = voided(marks, COLS_N).reshape(LANES, LANES).T
-    like = (
-        lax.rem(lax.broadcasted_iota(jnp.int32, (LANES, LANES), 0), 4)
-        == lax.rem(lax.broadcasted_iota(jnp.int32, (LANES, LANES), 1), 4)
-    )
-    w_group[0:LANES, :] = jnp.where(like & (target == sources), 1.0, 0.0).astype(bf16)
-    block_first = jnp.min(jnp.min(marks, 0), 0, keepdims=True)
-    block_last = jnp.max(jnp.max(marks, 0), 0, keepdims=True)
-    block_mark = jnp.where(head_half, block_first, block_last)
-    block_rows = jnp.where(like[:8] & (block_mark == sources[:8]), 1.0, 0.0)
-    w_group[LANES:, :] = jnp.concatenate([block_rows, jnp.zeros_like(block_rows)], 0).astype(bf16)
-    mark_b_send[...] = block_mark
-    mark_b[0] = jnp.full((8, LANES), -1.0, f32)
-    to_rows(mark_b_send, lambda o: mark_b.at[o], mark_sem.at[1])
-    first_range(5, 8)
-    settle(mark_b, ROWS_N - 1, mark_sem.at[1, 1])
-    marks_b = voided(mark_b[...], ROWS_N).reshape(8 * ROWS_N, LANES)
-    marks_b = jnp.concatenate([marks_b, jnp.full((LANES - 8 * ROWS_N, LANES), -1.0, f32)], 0)
-    block_sources = marks_b.T
-    w_block[...] = jnp.where(like & (mark_a[...].reshape(LANES, LANES) == block_sources), 1.0, 0.0).astype(bf16)
+    def group_weights():
+        settle(mark_a, COLS_N - 1, mark_sem.at[0, 1])
+        marks = mark_a[...]
+        target = marks.reshape(LANES, LANES)
+        sources = voided(marks, COLS_N).reshape(LANES, LANES).T
+        w_group[16:, :] = jnp.where(like & (target == sources), 1.0, 0.0).astype(bf16)
+        block_first = jnp.min(jnp.min(marks, 0), 0, keepdims=True)
+        block_last = jnp.max(jnp.max(marks, 0), 0, keepdims=True)
+        block_mark = jnp.where(head_half, block_first, block_last)
+        block_rows = jnp.where(like[:8] & (block_mark == sources[:8]), 1.0, 0.0)
+        w_group[0:16, :] = jnp.concatenate([block_rows, jnp.zeros_like(block_rows)], 0).astype(bf16)
+        mark_b_send[...] = block_mark
+        mark_b[0] = jnp.full((8, LANES), -1.0, f32)
+
+    def block_weights():
+        settle(mark_b, ROWS_N - 1, mark_sem.at[1, 1])
+        marks_b = voided(mark_b[...], ROWS_N).reshape(8 * ROWS_N, LANES)
+        marks_b = jnp.concatenate(
+            [marks_b, jnp.full((LANES - 8 * ROWS_N, LANES), -1.0, f32)], 0
+        )
+        target = mark_a[...].reshape(LANES, LANES)
+        w_block[...] = jnp.where(like & (target == marks_b.T), 1.0, 0.0).astype(bf16)
+
     for e in range(EXCHANGES):
         recv_b[e, 0] = jnp.zeros((8, LANES), f32)
 
@@ -243,14 +249,21 @@
             lambda o: recv_a.at[e, o],
             sem_a.at[e],
         )
+        if e == 0:
+            group_weights()
         settle(recv_a.at[e], COLS_N - 1, sem_a.at[e, 1])
-        group = select_sum(w_group[...], recv_a[e].reshape(LANES, LANES))
-        send_b[e] = group[LANES : LANES + 8]
+        parts = split3(recv_a[e].reshape(LANES, LANES))
+        send_b[e] = select_sum(w_group[0:16, :], parts)[:8]
         to_rows(send_b.at[e], lambda o: recv_b.at[e, o], sem_b.at[e])
+        if e == 0:
+            to_rows(mark_b_send, lambda o: mark_b.at[o], mark_sem.at[1])
+        group = select_sum(w_group[16:, :], parts)
         settle(recv_b.at[e], ROWS_N - 1, sem_b.at[e, 1])
+        if e == 0:
+            block_weights()
         blocks = recv_b[e].reshape(8 * ROWS_N, LANES)
         blocks = jnp.concatenate([blocks, jnp.zeros((LANES - 8 * ROWS_N, LANES), f32)], 0)
-        whole = group[:LANES] + select_sum(w_block[...], blocks)
+        whole = group + select_sum(w_block[...], split3(blocks))
         send_c[e] = whole.reshape(COLS_N, 8, LANES)
         recv_c[e, col] = send_c[e, 0]
         @pl.loop(1, COLS_N)
@@ -337,7 +350,9 @@
         def _(c):
             start = pl.multiple_of(c * CHUNK, CHUNK)
             x = x_ref[pl.ds(start, CHUNK), :]
-            s = lax.dot_general(frame, x, NT, preferred_element_type=f32)
+            s = lax.dot_general(
+                frame, xt_ref[:, pl.ds(start, CHUNK)], NN, preferred_element_type=f32
+            )
             rel = rel_of(start, CHUNK)
             pieces = [
                 jnp.where(
@@ -365,8 +380,9 @@
     @pl.loop(0, ROWS // CHUNK)
     def _(c):
         start = pl.multiple_of(c * CHUNK, CHUNK)
-        x = x_ref[pl.ds(start, CHUNK), :]
-        s = lax.dot_general(frame, x, NT, preferred_element_type=f32)
+        s = lax.dot_general(
+            frame, xt_ref[:, pl.ds(start, CHUNK)], NN, preferred_element_type=f32
+        )
         rel = rel_of(start, CHUNK)
         found = jnp.zeros((8, CHUNK), f32)
         for k in range(SLOTS):
@@ -394,6 +410,7 @@
         out_specs=vmem,
         scratch_shapes=[
             pltpu.VMEM((ROWS, WIDTH), bf16),
+            pltpu.VMEM((WIDTH, ROWS), bf16),
             pltpu.VMEM((144, WIDTH), f32),
             pltpu.VMEM((TILES, 64, LANES), f32),
             pltpu.VMEM((TILES, 64, LANES), f32),
@@ -418,10 +435,10 @@
             DMA((EXCHANGES, 2)),
         ],
         compiler_params=pltpu.CompilerParams(
-            collective_id=0, has_side_effects=True, vmem_limit_bytes=56 * 2**20
+            collective_id=0, has_side_effects=True, vmem_limit_bytes=53 * 2**20
         ),
         name="principal_axes",
-    )(points, node_of_row.reshape(1, ROWS), init_axes)
+    )(points, node_of_row.reshape(1, ROWS), init_axes.T)
 
 
 def solution(mesh):

time: 82.6 us -> 71 us (0.86)
  Pallas kernels: 79.1 us -> 68.6 us
  local copies, waits for them, and re-layouts: 3.31 us -> 2.2 us
    pallas_call x1, Pallas kernels: 79.1 us -> 68.6 us  [shards(): pl.pallas_call(kernel, out_shape=jax.ShapeDtypeStruct((AXES, ROWS), f32),...]
    unnamed x2 -> x5, local copies, waits for them, and re-layouts: 3.31 us -> 2.2 us
where the time goes in v2:
time: 71 us; the launch traced here: 70.8 us
  Pallas kernels  68.6 us (97%)
  local copies, waits for them, and re-layouts  2.2 us (3%)
    pallas_call x1, Pallas kernels, shards(): pl.pallas_call(kernel, out_shape=jax.ShapeDtypeStruct((AXES, ROWS), f32),...  68.6 us
    unnamed x5, local copies, waits for them, and re-layouts  2.2 us

profile of v2, /device:TPU:1, one launch (start us, length us, event | category | flops | bytes accessed | tf_op | source)
XLA Modules:
  0.0 70.8 jit_solution(9966337877488200062)
XLA Ops:
  0.0 0.0 copy-start
  0.0 0.8 %copy-done = s32[8192]{0:T(1024)S(1)} copy-done((s32[8192]{0:T(1024)S(1)}, s32[8192]{0:T(1024)}, u32[]{:S(2)}) %copy-start) | copy-done | bytes 32792
  0.8 0.0 copy-start.1
  0.8 0.7 %copy-done.1 = f32[768,8]{0,1:T(8,128)S(1)} copy-done((f32[768,8]{0,1:T(8,128)S(1)}, f32[768,8]{0,1:T(8,128)}, u32[]{:S(2)}) %copy-start.1) | copy-done | bytes 24600
  1.5 68.6 %principal_axes.1 = f32[8,8192]{1,0:T(8,128)S(1)} custom-call(bf16[8192,768]{1,0:T(8,128)(2,1)} %points_ref.1, s32[1,8192]{1,0:T(1,128)S(1)} %bitcast.2, f32[8,768]{1,0:T(8,128)S(1)} %bitcast.3), custom_call_target="tpu_custom_call" | custom-call | tf_op jit(solution)/shard_map/principal_axes/pallas_call | solution.py:406
  70.1 0.7 copy.5
Async XLA Ops:
  0.0 0.8 %copy-start = (s32[8192]{0:T(1024)S(1)}, s32[8192]{0:T(1024)}, u32[]{:S(2)}) copy-start(s32[8192]{0:T(1024)} %param.4) | copy-start | bytes 98308
  0.8 0.7 %copy-start.1 = (f32[768,8]{0,1:T(8,128)S(1)}, f32[768,8]{0,1:T(8,128)}, u32[]{:S(2)}) copy-start(f32[768,8]{0,1:T(8,128)} %param.5) | copy-start | bytes 73732

commit v3 on v2

--- a/solution.py
+++ b/solution.py
@@ -16,8 +16,18 @@
 LANES = 128
 TILES = WIDTH // LANES
 LOAD = 1024
+FIRST = 2048
 CHUNK = 4096
 EXCHANGES = 3
+SIDE = 4
+
+
+def hops(o):
+    return min(o, SIDE - o)
+
+
+FAR_COLS = sorted(range(1, COLS_N), key=lambda o: -hops(o // SIDE) - hops(o % SIDE))
+FAR_ROWS = sorted(range(1, ROWS_N), key=lambda o: -hops(o // 2))
 f32 = jnp.float32
 bf16 = jnp.bfloat16
 NT = (((1,), (1,)), ((), ()))
@@ -80,33 +90,34 @@
 
     barrier = pltpu.get_barrier_semaphore()
 
-    @pl.loop(1, COLS_N)
-    def _(o):
+    def col_at(o, sign=1):
+        x = lax.rem(col // SIDE + sign * (o // SIDE) + SIDE, SIDE)
+        z = lax.rem(lax.rem(col, SIDE) + sign * (o % SIDE) + SIDE, SIDE)
+        return x * SIDE + z
+
+    for o in FAR_COLS:
         pl.semaphore_signal(
-            barrier, inc=1, device_id=(row, lax.rem(col + o, COLS_N)), device_id_type=MESH
-        )
-
-    @pl.loop(1, ROWS_N)
-    def _(o):
+            barrier, inc=1, device_id=(row, col_at(o)), device_id_type=MESH
+        )
+
+    for o in FAR_ROWS:
         pl.semaphore_signal(
             barrier, inc=1, device_id=(lax.rem(row + o, ROWS_N), col), device_id_type=MESH
         )
 
     def to_cols(source, target, sems):
-        @pl.loop(1, COLS_N)
-        def _(o):
+        for o in FAR_COLS:
             pltpu.make_async_remote_copy(
                 src_ref=source(o),
                 dst_ref=target(o),
                 send_sem=sems.at[0],
                 recv_sem=sems.at[1],
-                device_id=(row, lax.rem(col + o, COLS_N)),
+                device_id=(row, col_at(o)),
                 device_id_type=MESH,
             ).start()
 
     def to_rows(source, target, sems):
-        @pl.loop(1, ROWS_N)
-        def _(o):
+        for o in FAR_ROWS:
             pltpu.make_async_remote_copy(
                 src_ref=source,
                 dst_ref=target(o),
@@ -143,17 +154,19 @@
             total = total + value[:, t * LANES : (t + 1) * LANES]
         return total
 
-    def first_pass(c):
-        load(c).wait()
+    def first_pass(c, n):
+        FIRST = n * LOAD
+        for part in range(n):
+            load(c + part).wait()
         start = pl.multiple_of(c * LOAD, LOAD)
-        x = x_ref[pl.ds(start, LOAD), :]
+        x = x_ref[pl.ds(start, FIRST), :]
         xt = x.T
-        xt_ref[:, pl.ds(start, LOAD)] = xt
+        xt_ref[:, pl.ds(start, FIRST)] = xt
         s = lax.dot_general(base_pad, xt, NN, preferred_element_type=f32)[:8]
         high = s.astype(bf16).astype(f32)
         low = s - high
-        rel = rel_of(start, LOAD)
-        sub_wide = lax.broadcasted_iota(jnp.int32, (8, LOAD), 0)
+        rel = rel_of(start, FIRST)
+        sub_wide = lax.broadcasted_iota(jnp.int32, (8, FIRST), 0)
         member = jnp.where(rel == sub_wide, 1.0, 0.0)
         pieces = [jnp.where(rel == k, high, 0.0) for k in range(SLOTS)]
         pieces += [jnp.where(rel == k, low, 0.0) for k in range(SLOTS)]
@@ -163,14 +176,16 @@
         colsum_ref[0:8, :] += lane_sum(member)
 
     def first_range(lower, upper):
-        @pl.loop(lower, upper)
+        first_pass(0, 1)
+        first_pass(1, 1)
+
+        @pl.loop(1, 4)
         def _(c):
-            first_pass(c)
-
-    first_range(0, 2)
+            first_pass(2 * c, 2)
+
+    first_range(0, ROWS // FIRST)
     pl.semaphore_wait(barrier, COLS_N - 1 + ROWS_N - 1)
     to_cols(lambda o: mark_a.at[0], lambda o: mark_a.at[o], mark_sem.at[0])
-    first_range(2, ROWS // LOAD)
     like = (
         lax.rem(lax.broadcasted_iota(jnp.int32, (LANES, LANES), 0), 4)
         == lax.rem(lax.broadcasted_iota(jnp.int32, (LANES, LANES), 1), 4)
@@ -245,7 +260,7 @@
     def exchange(e):
         recv_a[e, 0] = send_a[e, col]
         to_cols(
-            lambda o: send_a.at[e, lax.rem(col + o, COLS_N)],
+            lambda o: send_a.at[e, col_at(o)],
             lambda o: recv_a.at[e, o],
             sem_a.at[e],
         )
@@ -266,14 +281,13 @@
         whole = group + select_sum(w_block[...], split3(blocks))
         send_c[e] = whole.reshape(COLS_N, 8, LANES)
         recv_c[e, col] = send_c[e, 0]
-        @pl.loop(1, COLS_N)
-        def _(o):
+        for o in FAR_COLS:
             pltpu.make_async_remote_copy(
                 src_ref=send_c.at[e, o],
                 dst_ref=recv_c.at[e, col],
                 send_sem=sem_c.at[e, 0],
                 recv_sem=sem_c.at[e, 1],
-                device_id=(row, lax.rem(col - o + COLS_N, COLS_N)),
+                device_id=(row, col_at(o, -1)),
                 device_id_type=MESH,
             ).start()
         settle(recv_c.at[e], COLS_N - 1, sem_c.at[e, 1])

time: 71 us -> 68 us (0.958)
  Pallas kernels: 68.6 us -> 65.6 us
    pallas_call x1, Pallas kernels: 68.6 us -> 65.6 us  [shards(): pl.pallas_call(kernel, out_shape=jax.ShapeDtypeStruct((AXES, ROWS), f32),...]
where the time goes in v3:
time: 68 us; the launch traced here: 67.8 us
  Pallas kernels  65.6 us (96%)
  local copies, waits for them, and re-layouts  2.2 us (3%)
    pallas_call x1, Pallas kernels, shards(): pl.pallas_call(kernel, out_shape=jax.ShapeDtypeStruct((AXES, ROWS), f32),...  65.6 us
    unnamed x5, local copies, waits for them, and re-layouts  2.2 us

profile of v3, /device:TPU:1, one launch (start us, length us, event | category | flops | bytes accessed | tf_op | source)
XLA Modules:
  0.0 67.8 jit_solution(8025105797939398728)
XLA Ops:
  0.0 0.0 copy-start
  0.0 0.8 %copy-done = s32[8192]{0:T(1024)S(1)} copy-done((s32[8192]{0:T(1024)S(1)}, s32[8192]{0:T(1024)}, u32[]{:S(2)}) %copy-start) | copy-done | bytes 32792
  0.8 0.0 copy-start.1
  0.8 0.7 %copy-done.1 = f32[768,8]{0,1:T(8,128)S(1)} copy-done((f32[768,8]{0,1:T(8,128)S(1)}, f32[768,8]{0,1:T(8,128)}, u32[]{:S(2)}) %copy-start.1) | copy-done | bytes 24600
  1.5 65.6 %principal_axes.1 = f32[8,8192]{1,0:T(8,128)S(1)} custom-call(bf16[8192,768]{1,0:T(8,128)(2,1)} %points_ref.1, s32[1,8192]{1,0:T(1,128)S(1)} %bitcast.2, f32[8,768]{1,0:T(8,128)S(1)} %bitcast.3), custom_call_target="tpu_custom_call" | custom-call | tf_op jit(solution)/shard_map/principal_axes/pallas_call | solution.py:420
  67.1 0.7 %copy.5 = f32[8,8192]{1,0:T(8,128)} copy(f32[8,8192]{1,0:T(8,128)S(1)} %principal_axes.1) | data formatting | bytes 524288
Async XLA Ops:
  0.0 0.8 %copy-start = (s32[8192]{0:T(1024)S(1)}, s32[8192]{0:T(1024)}, u32[]{:S(2)}) copy-start(s32[8192]{0:T(1024)} %param.4) | copy-start | bytes 98308
  0.8 0.7 %copy-start.1 = (f32[768,8]{0,1:T(8,128)S(1)}, f32[768,8]{0,1:T(8,128)}, u32[]{:S(2)}) copy-start(f32[768,8]{0,1:T(8,128)} %param.5) | copy-start | bytes 73732

commit v4 on v3

--- a/solution.py
+++ b/solution.py
@@ -65,7 +65,12 @@
     mark_b,
     mark_b_send,
     w_group,
-    w_block,
+    near_own,
+    cross_own,
+    near_block,
+    cross_block,
+    near_ref,
+    cross_ref,
     send_a,
     recv_a,
     send_b,
@@ -201,23 +206,31 @@
         marks = mark_a[...]
         target = marks.reshape(LANES, LANES)
         sources = voided(marks, COLS_N).reshape(LANES, LANES).T
-        w_group[16:, :] = jnp.where(like & (target == sources), 1.0, 0.0).astype(bf16)
+        w_group[...] = jnp.where(like & (target == sources), 1.0, 0.0).astype(bf16)
         block_first = jnp.min(jnp.min(marks, 0), 0, keepdims=True)
         block_last = jnp.max(jnp.max(marks, 0), 0, keepdims=True)
         block_mark = jnp.where(head_half, block_first, block_last)
-        block_rows = jnp.where(like[:8] & (block_mark == sources[:8]), 1.0, 0.0)
-        w_group[0:16, :] = jnp.concatenate([block_rows, jnp.zeros_like(block_rows)], 0).astype(bf16)
+        usable = voided(marks, COLS_N)
+        wide = jnp.broadcast_to(block_mark[None], (COLS_N, 8, LANES))
+        other = pltpu.roll(block_mark, 4, 0)
+        near_own[...] = jnp.where(marks == wide, 1.0, 0.0)
+        cross_own[...] = jnp.where(
+            (marks == jnp.broadcast_to(other[None], marks.shape))
+            & jnp.broadcast_to((other != block_mark)[None], marks.shape),
+            1.0,
+            0.0,
+        )
+        near_ref[...] = jnp.where(usable == wide, 1.0, 0.0)
+        cross_ref[...] = jnp.where(pltpu.roll(usable, 4, 1) == wide, 1.0, 0.0)
         mark_b_send[...] = block_mark
         mark_b[0] = jnp.full((8, LANES), -1.0, f32)
 
     def block_weights():
         settle(mark_b, ROWS_N - 1, mark_sem.at[1, 1])
-        marks_b = voided(mark_b[...], ROWS_N).reshape(8 * ROWS_N, LANES)
-        marks_b = jnp.concatenate(
-            [marks_b, jnp.full((LANES - 8 * ROWS_N, LANES), -1.0, f32)], 0
-        )
-        target = mark_a[...].reshape(LANES, LANES)
-        w_block[...] = jnp.where(like & (target == marks_b.T), 1.0, 0.0).astype(bf16)
+        usable = voided(mark_b[...], ROWS_N)
+        wide = jnp.broadcast_to(mark_b_send[...][None], (ROWS_N, 8, LANES))
+        near_block[...] = jnp.where(usable == wide, 1.0, 0.0)
+        cross_block[...] = jnp.where(pltpu.roll(usable, 4, 1) == wide, 1.0, 0.0)
 
     for e in range(EXCHANGES):
         recv_b[e, 0] = jnp.zeros((8, LANES), f32)
@@ -267,19 +280,26 @@
         if e == 0:
             group_weights()
         settle(recv_a.at[e], COLS_N - 1, sem_a.at[e, 1])
-        parts = split3(recv_a[e].reshape(LANES, LANES))
-        send_b[e] = select_sum(w_group[0:16, :], parts)[:8]
+        tiles = recv_a[e]
+        send_b[e] = jnp.sum(near_ref[...] * tiles, 0) + jnp.sum(
+            cross_ref[...] * pltpu.roll(tiles, 4, 1), 0
+        )
         to_rows(send_b.at[e], lambda o: recv_b.at[e, o], sem_b.at[e])
         if e == 0:
             to_rows(mark_b_send, lambda o: mark_b.at[o], mark_sem.at[1])
-        group = select_sum(w_group[16:, :], parts)
+        group = select_sum(w_group[...], split3(tiles.reshape(LANES, LANES)))
         settle(recv_b.at[e], ROWS_N - 1, sem_b.at[e, 1])
         if e == 0:
             block_weights()
-        blocks = recv_b[e].reshape(8 * ROWS_N, LANES)
-        blocks = jnp.concatenate([blocks, jnp.zeros((LANES - 8 * ROWS_N, LANES), f32)], 0)
-        whole = group + select_sum(w_block[...], split3(blocks))
-        send_c[e] = whole.reshape(COLS_N, 8, LANES)
+        blocks = recv_b[e]
+        outer = jnp.sum(near_block[...] * blocks, 0) + jnp.sum(
+            cross_block[...] * pltpu.roll(blocks, 4, 1), 0
+        )
+        send_c[e] = (
+            group.reshape(COLS_N, 8, LANES)
+            + near_own[...] * outer[None]
+            + cross_own[...] * pltpu.roll(outer, 4, 0)[None]
+        )
         recv_c[e, col] = send_c[e, 0]
         for o in FAR_COLS:
             pltpu.make_async_remote_copy(
@@ -391,20 +411,20 @@
 
     frame = frame_used()
 
-    @pl.loop(0, ROWS // CHUNK)
+    @pl.loop(0, 1)
     def _(c):
-        start = pl.multiple_of(c * CHUNK, CHUNK)
+        start = pl.multiple_of(c * ROWS, ROWS)
         s = lax.dot_general(
-            frame, xt_ref[:, pl.ds(start, CHUNK)], NN, preferred_element_type=f32
-        )
-        rel = rel_of(start, CHUNK)
-        found = jnp.zeros((8, CHUNK), f32)
+            frame, xt_ref[:, pl.ds(start, ROWS)], NN, preferred_element_type=f32
+        )
+        rel = rel_of(start, ROWS)
+        found = jnp.zeros((8, ROWS), f32)
         for k in range(SLOTS):
             centred = s[8 * k : 8 * k + 8] - jnp.broadcast_to(
-                offset_ref[8 * k : 8 * k + 8, 0:1], (8, CHUNK)
+                offset_ref[8 * k : 8 * k + 8, 0:1], (8, ROWS)
             )
             found = jnp.where(rel == k, centred, found)
-        out_ref[:, pl.ds(start, CHUNK)] = found
+        out_ref[:, pl.ds(start, ROWS)] = found
 
     settle(mark_a, COLS_N - 1, mark_sem.at[0, 0])
     settle(mark_b, ROWS_N - 1, mark_sem.at[1, 0])
@@ -434,8 +454,13 @@
             pltpu.VMEM((COLS_N, 8, LANES), f32),
             pltpu.VMEM((ROWS_N, 8, LANES), f32),
             pltpu.VMEM((8, LANES), f32),
-            pltpu.VMEM((144, LANES), bf16),
             pltpu.VMEM((LANES, LANES), bf16),
+            pltpu.VMEM((COLS_N, 8, LANES), f32),
+            pltpu.VMEM((COLS_N, 8, LANES), f32),
+            pltpu.VMEM((ROWS_N, 8, LANES), f32),
+            pltpu.VMEM((ROWS_N, 8, LANES), f32),
+            pltpu.VMEM((COLS_N, 8, LANES), f32),
+            pltpu.VMEM((COLS_N, 8, LANES), f32),
             pltpu.VMEM((EXCHANGES, COLS_N, 8, LANES), f32),
             pltpu.VMEM((EXCHANGES, COLS_N, 8, LANES), f32),
             pltpu.VMEM((EXCHANGES, 8, LANES), f32),

time: 68 us -> 66.9 us (0.984)
  Pallas kernels: 65.6 us -> 64.4 us
    pallas_call x1, Pallas kernels: 65.6 us -> 64.4 us  [shards(): pl.pallas_call(kernel, out_shape=jax.ShapeDtypeStruct((AXES, ROWS), f32),...]
where the time goes in v4:
time: 66.9 us; the launch traced here: 66.6 us
  Pallas kernels  64.4 us (96%)
  local copies, waits for them, and re-layouts  2.2 us (3%)
    pallas_call x1, Pallas kernels, shards(): pl.pallas_call(kernel, out_shape=jax.ShapeDtypeStruct((AXES, ROWS), f32),...  64.4 us
    unnamed x5, local copies, waits for them, and re-layouts  2.2 us

profile of v4, /device:TPU:1, one launch (start us, length us, event | category | flops | bytes accessed | tf_op | source)
XLA Modules:
  0.0 66.6 jit_solution(5304769141982126501)
XLA Ops:
  0.0 0.0 copy-start
  0.0 0.8 %copy-done = s32[8192]{0:T(1024)S(1)} copy-done((s32[8192]{0:T(1024)S(1)}, s32[8192]{0:T(1024)}, u32[]{:S(2)}) %copy-start) | copy-done | bytes 32792
  0.8 0.0 copy-start.1
  0.8 0.7 %copy-done.1 = f32[768,8]{0,1:T(8,128)S(1)} copy-done((f32[768,8]{0,1:T(8,128)S(1)}, f32[768,8]{0,1:T(8,128)}, u32[]{:S(2)}) %copy-start.1) | copy-done | bytes 24600
  1.5 64.4 %principal_axes.1 = f32[8,8192]{1,0:T(8,128)S(1)} custom-call(bf16[8192,768]{1,0:T(8,128)(2,1)} %points_ref.1, s32[1,8192]{1,0:T(1,128)S(1)} %bitcast.2, f32[8,768]{1,0:T(8,128)S(1)} %bitcast.3), custom_call_target="tpu_custom_call" | custom-call | tf_op jit(solution)/shard_map/principal_axes/pallas_call | solution.py:440
  65.9 0.7 %copy.5 = f32[8,8192]{1,0:T(8,128)} copy(f32[8,8192]{1,0:T(8,128)S(1)} %principal_axes.1) | data formatting | bytes 524288
Async XLA Ops:
  0.0 0.8 %copy-start = (s32[8192]{0:T(1024)S(1)}, s32[8192]{0:T(1024)}, u32[]{:S(2)}) copy-start(s32[8192]{0:T(1024)} %param.4) | copy-start | bytes 98308
  0.8 0.7 %copy-start.1 = (f32[768,8]{0,1:T(8,128)S(1)}, f32[768,8]{0,1:T(8,128)}, u32[]{:S(2)}) copy-start(f32[768,8]{0,1:T(8,128)} %param.5) | copy-start | bytes 73732

commit v5 on v4

--- a/solution.py
+++ b/solution.py
@@ -184,13 +184,18 @@
         first_pass(0, 1)
         first_pass(1, 1)
 
-        @pl.loop(1, 4)
+        @pl.loop(1, 3)
         def _(c):
             first_pass(2 * c, 2)
 
     first_range(0, ROWS // FIRST)
     pl.semaphore_wait(barrier, COLS_N - 1 + ROWS_N - 1)
     to_cols(lambda o: mark_a.at[0], lambda o: mark_a.at[o], mark_sem.at[0])
+
+    @pl.loop(3, 4)
+    def _(c):
+        first_pass(2 * c, 2)
+
     like = (
         lax.rem(lax.broadcasted_iota(jnp.int32, (LANES, LANES), 0), 4)
         == lax.rem(lax.broadcasted_iota(jnp.int32, (LANES, LANES), 1), 4)
@@ -338,7 +343,7 @@
             vector = vectors[k]
             square = jnp.sum(vector * vector, 1, keepdims=True)
             square = jnp.where(live[:, 0:1], square, 1.0)
-            inverse = 1.0 / square
+            inverse = pl.reciprocal(square)
             for j in range(k + 1, AXES):
                 along = jnp.sum(vector * vectors[j], 1, keepdims=True) * inverse
                 vectors[j] = vectors[j] - along * vector

time: 66.9 us -> 66.6 us (level)
  no operation moved by 1% of the time
where the time goes in v5:
time: 66.6 us; the launch traced here: 66.4 us
  Pallas kernels  64.2 us (96%)
  local copies, waits for them, and re-layouts  2.2 us (3%)
    pallas_call x1, Pallas kernels, shards(): pl.pallas_call(kernel, out_shape=jax.ShapeDtypeStruct((AXES, ROWS), f32),...  64.2 us
    unnamed x5, local copies, waits for them, and re-layouts  2.2 us

profile of v5, /device:TPU:1, one launch (start us, length us, event | category | flops | bytes accessed | tf_op | source)
XLA Modules:
  0.0 66.4 jit_solution(4673268293502868468)
XLA Ops:
  0.0 0.0 copy-start
  0.0 0.8 %copy-done = s32[8192]{0:T(1024)S(1)} copy-done((s32[8192]{0:T(1024)S(1)}, s32[8192]{0:T(1024)}, u32[]{:S(2)}) %copy-start) | copy-done | bytes 32792
  0.8 0.0 copy-start.1
  0.8 0.7 %copy-done.1 = f32[768,8]{0,1:T(8,128)S(1)} copy-done((f32[768,8]{0,1:T(8,128)S(1)}, f32[768,8]{0,1:T(8,128)}, u32[]{:S(2)}) %copy-start.1) | copy-done | bytes 24600
  1.5 64.2 %principal_axes.1 = f32[8,8192]{1,0:T(8,128)S(1)} custom-call(bf16[8192,768]{1,0:T(8,128)(2,1)} %points_ref.1, s32[1,8192]{1,0:T(1,128)S(1)} %bitcast.2, f32[8,768]{1,0:T(8,128)S(1)} %bitcast.3), custom_call_target="tpu_custom_call" | custom-call | tf_op jit(solution)/shard_map/principal_axes/pallas_call | solution.py:445
  65.7 0.7 %copy.5 = f32[8,8192]{1,0:T(8,128)} copy(f32[8,8192]{1,0:T(8,128)S(1)} %principal_axes.1) | data formatting | bytes 524288
Async XLA Ops:
  0.0 0.8 %copy-start = (s32[8192]{0:T(1024)S(1)}, s32[8192]{0:T(1024)}, u32[]{:S(2)}) copy-start(s32[8192]{0:T(1024)} %param.4) | copy-start | bytes 98308
  0.8 0.7 %copy-start.1 = (f32[768,8]{0,1:T(8,128)S(1)}, f32[768,8]{0,1:T(8,128)}, u32[]{:S(2)}) copy-start(f32[768,8]{0,1:T(8,128)} %param.5) | copy-start | bytes 73732
